TPU v7x, 32 devices: a whole 2x2x4 slice. The times are simulated.
32 devices in a mesh: grp: 8 (over y, x, core), top: 4 (over z).
Axes of the slice: x: 2, y: 2, z: 4, core: 2. Of those that a mesh axis runs over, the one named last changes fastest.
Arguments:
- basis_grad: float32 [8, 4, 512, 384], P('grp', 'top'), may hold values from -6 to 6
- leaf_q: float32 [8, 4, 512, 384], P('grp', 'top'), may hold values from -0.25 to 0.25
- leaf_rinv: float32 [8, 4, 384, 384], P('grp', 'top'), may hold values from -5 to 4, as said below
- merge_q1: float32 [8, 4, 384, 384], P('grp', 'top'), may hold values from -0.3125 to 0.3125
- merge_q2: float32 [4, 384, 384], P('top', 'grp'), may hold values from -0.15625 to 0.15625
Outputs:
- data_grad: float32 [8, 4, 512, 384], P('grp', 'top')
Inputs may be any that keep to these rules, and one draw needn't show every extreme that they name: Each leaf_rinv[i,g] is upper triangular with a diagonal between 1 and 4.
All inputs are finite; a program needn't handle non-finite values.
Results may differ from a plain program's by a relative error of at most 0.00023.
Values sent between devices are 32-bit elements; how exact they have to be, the bound alone decides.
A program may use at most 64 MiB of HBM per device.

v0:
```python
import jax
import jax.numpy as jnp
from jax import lax
from jax.sharding import PartitionSpec as P


def product(former, latter, former_dim, latter_dim):
    return lax.dot_general(
        former,
        latter,
        (((former_dim,), (latter_dim,)), ((), ())),
        precision=lax.Precision.HIGH,
        preferred_element_type=jnp.float32,
    )


def symmetrize(matrix):
    return jnp.tril(matrix) + jnp.tril(matrix, -1).T


def per_device(basis_grad, leaf_q, leaf_rinv, merge_q1, merge_q2):
    cotangent = basis_grad[0, 0]
    leaf_basis = leaf_q[0, 0]
    inverse = leaf_rinv[0, 0]
    first_block = merge_q1[0, 0]
    second_factor = lax.all_gather(merge_q2[0], "grp", axis=0, tiled=True)
    projected = product(leaf_basis, cotangent, 0, 0)
    combined = product(first_block, second_factor, 1, 0)
    top_adjoint = -lax.psum(product(projected, combined, 0, 0), ("grp", "top"))
    top_sym = symmetrize(top_adjoint)
    spread = product(leaf_basis, combined, 1, 0)
    outer = product(inverse, combined, 1, 0)
    inner = cotangent + product(spread, top_sym, 1, 0)
    result = product(inner, outer, 1, 1)
    return result[None, None]


def solution(mesh):
    placed = (
        P("grp", "top", None, None),
        P("grp", "top", None, None),
        P("grp", "top", None, None),
        P("grp", "top", None, None),
        P("top", "grp", None),
    )
    return jax.shard_map(
        per_device,
        mesh=mesh,
        in_specs=placed,
        out_specs=P("grp", "top", None, None),
        check_vma=False,
    )
```

profile of v0, /device:TPU:0, one launch (start us, length us, event | category | flops | bytes accessed | tf_op | source)
XLA Modules:
  0.0 163.3 jit_solution(13517483141683757118)
XLA Ops:
  6.5 0.0 copy-start
  6.5 0.0 copy-start.2
  6.5 0.0 all-reduce.2.cloned.1.call-start
  6.5 11.9 %all-gather = f32[1,384,384]{2,1,0:T(8,128)S(1)} all-gather(f32[1,48,384]{2,1,0:T(8,128)} %param.9), channel_id=2, replica_groups=mesh['grp'=8,'top'=4] {'grp'}, dimensions={1}, use_global_device_ids=true | all-gather | bytes 663552 | tf_op jit(solution)/shard_map/all_gather | solution.py:26
  18.4 0.0 copy-done.2
  18.4 0.0 copy-start.1
  18.4 0.7 fusion.7
  19.2 0.0 copy-done
  19.2 0.4 copy-done.1
  19.6 0.8 fusion
  20.4 1.6 fusion.17
  22.0 0.0 copy-start.3
  22.0 0.0 all-reduce.2.cloned.1.call-update
  22.0 1.0 copy-done.3
  23.0 1.1 fusion.5
  24.2 1.2 fusion.2
  25.3 124.4 %all-reduce.2.cloned.1.call-done = f32[384,384]{1,0:T(8,128)} async-done(((f32[384,384]{1,0:T(8,128)}), f32[384,384]{1,0:T(8,128)}) %all-reduce.2.cloned.1.call-update) | async-done | bytes 589840 | tf_op jit(solution)/shard_map/psum | solution.py:29
  149.8 1.1 neg.3
  150.9 1.1 copy.6
  151.9 2.7 %convolution_add_fusion = f32[512,384]{1,0:T(8,128)S(1)} fusion(f32[384,512]{1,0:T(8,128)S(1)} %fusion.2, f32[1,1,512,384]{3,2,1,0:T(8,128)S(1)} %copy-done.1, f32[384,384]{0,1:T(8,128)} %copy.6, s32[384]{0:T(512)S(1)} %iota_add_fusion, f32[384,384]{1,0:T(8,128)} %all-reduce.2.cloned.1.call-done), kind=kOutput, calls=%fused_computation.1 | convolution fusion | flops 454066176 | bytes 3540480 | tf_op jit(solution)/shard_map/dot_general | solution.py:8
  154.7 1.8 %convolution_bitcast_fusion = f32[1,1,512,384]{3,2,1,0:T(8,128)} fusion(f32[512,384]{1,0:T(8,128)S(1)} %convolution_add_fusion, f32[384,384]{1,0:T(8,128)S(1)} %fusion.5), kind=kOutput, calls=%fused_computation | convolution fusion | flops 452984832 | bytes 2162688 | tf_op jit(solution)/shard_map/dot_general | solution.py:8
  (1 shorter events, 0.0 us)
Async XLA Ops:
  6.5 12.6 %copy-start = (f32[1,1,512,384]{3,2,1,0:T(8,128)S(1)}, f32[1,1,512,384]{3,2,1,0:T(8,128)}, u32[]{:S(2)}) copy-start(f32[1,1,512,384]{3,2,1,0:T(8,128)} %param.6) | copy-start | bytes 2359300
  6.5 11.9 %copy-start.2 = (f32[1,1,384,384]{3,2,1,0:T(8,128)S(1)}, f32[1,1,384,384]{3,2,1,0:T(8,128)}, u32[]{:S(2)}) copy-start(f32[1,1,384,384]{3,2,1,0:T(8,128)} %param.8) | copy-start | bytes 1769476
  6.5 143.2 %all-reduce.2.cloned.1.call-start = ((), (), s32[]{:S(2)}) async-start(), calls=%async_computation | async-start | bytes 1179648 | tf_op jit(solution)/shard_map/psum | solution.py:29
  18.4 1.1 copy-start.1
  22.0 1.1 copy-start.3
Sparse Core Ops, SparseCore 0:
  22.1 127.6 all-reduce.1
where the time goes:
time: 164 us; the launch traced here: 163 us
  waiting for transfers between devices  124 us (76%)
  between operations  13.4 us (8%)
  blocking collectives  11.9 us (7%)
  matrix products  9.86 us (6%)
  local copies, waits for them, and re-layouts  2.51 us (2%)
    psum x1, waiting for transfers between devices, per_device(): top_adjoint = -lax.psum(product(projected, combined, 0, 0), ('grp', 'top'))  124 us
    all_gather x1, blocking collectives, per_device(): second_factor = lax.all_gather(merge_q2[0], 'grp', axis=0, tiled=True)  11.9 us
    dot_general x7, matrix products, product(): lax.dot_general(former, latter, (((former_dim,), (latter_dim,)), ((), ())...  9.86 us
  transfers between devices with their start and end apart: 1, of which 1 were waited for; matrix products, arithmetic and copies ran while one was open for 1% of the time, Pallas kernels for 0%

commit v1 on v0

--- a/solution.py
+++ b/solution.py
@@ -2,6 +2,11 @@
 import jax.numpy as jnp
 from jax import lax
 from jax.sharding import PartitionSpec as P
+
+
+def by_each_axis(x, one, other):
+    partial = lax.psum(x, one)
+    return lax.psum(partial, other)
 
 
 def product(former, latter, former_dim, latter_dim):
@@ -26,7 +31,7 @@
     second_factor = lax.all_gather(merge_q2[0], "grp", axis=0, tiled=True)
     projected = product(leaf_basis, cotangent, 0, 0)
     combined = product(first_block, second_factor, 1, 0)
-    top_adjoint = -lax.psum(product(projected, combined, 0, 0), ("grp", "top"))
+    top_adjoint = -by_each_axis(product(projected, combined, 0, 0), "top", "grp")
     top_sym = symmetrize(top_adjoint)
     spread = product(leaf_basis, combined, 1, 0)
     outer = product(inverse, combined, 1, 0)

time: 164 us -> 133 us (0.81)
  waiting for transfers between devices: 124 us -> 94 us
    psum x1 -> x2, waiting for transfers between devices: 124 us -> 94 us  [the longest x1 56.6 us: by_each_axis(): return lax.psum(partial, other)]
  transfers between devices with their start and end apart: 1 -> 2, of which waited for: 1 -> 2; matrix products, arithmetic and copies ran while one was open for 1% -> 2% of each run, Pallas kernels for 0% -> 0%
where the time goes in v1:
time: 133 us
  waiting for transfers between devices  94 us (71%)
  between operations  13.5 us (10%)
  blocking collectives  11.9 us (9%)
  matrix products  9.86 us (7%)
  local copies, waits for them, and re-layouts  2.46 us (2%)
    psum x1, waiting for transfers between devices, by_each_axis(): return lax.psum(partial, other)  56.6 us
    psum x1, waiting for transfers between devices, by_each_axis(): partial = lax.psum(x, one)  37.4 us
    all_gather x1, blocking collectives, per_device(): second_factor = lax.all_gather(merge_q2[0], 'grp', axis=0, tiled=True)  11.9 us
    dot_general x7, matrix products, product(): lax.dot_general(former, latter, (((former_dim,), (latter_dim,)), ((), ())...  9.86 us
  transfers between devices with their start and end apart: 2, of which 2 were waited for; matrix products, arithmetic and copies ran while one was open for 2% of the time, Pallas kernels for 0%

profile of v1, /device:TPU:0, one launch (start us, length us, event | category | flops | bytes accessed | tf_op | source)
XLA Modules:
  0.0 132.8 jit_solution(1810101101500457952)
XLA Ops:
  6.5 0.0 copy-start
  6.5 0.0 copy-start.2
  6.5 0.0 all-reduce.3.cloned.1.call-start
  6.5 11.9 %all-gather = f32[1,384,384]{2,1,0:T(8,128)S(1)} all-gather(f32[1,48,384]{2,1,0:T(8,128)} %param.9), channel_id=2, replica_groups=mesh['grp'=8,'top'=4] {'grp'}, dimensions={1}, use_global_device_ids=true | all-gather | bytes 663552 | tf_op jit(solution)/shard_map/all_gather | solution.py:31
  18.4 0.0 copy-done.2
  18.4 0.0 copy-start.1
  18.4 0.7 fusion.7
  19.2 0.0 copy-done
  19.2 0.4 copy-done.1
  19.6 0.8 fusion
  20.4 1.6 %fusion.17 = f32[384,384]{1,0:T(8,128)} fusion(f32[384,384]{1,0:T(8,128)S(1)} %fusion, f32[384,384]{1,0:T(8,128)S(1)} %fusion.7), kind=kOutput, calls=%fused_computation.23 | convolution fusion | flops 339738624 | bytes 1769472 | tf_op jit(solution)/shard_map/dot_general | solution.py:13
  22.0 0.0 copy-start.3
  22.0 0.0 all-reduce.3.cloned.1.call-update
  22.0 0.0 all-reduce.5.cloned.1.call-start
  22.1 1.0 copy-done.3
  23.0 1.1 fusion.5
  24.2 37.4 %all-reduce.3.cloned.1.call-done = f32[384,384]{1,0:T(8,128)} async-done(((f32[384,384]{1,0:T(8,128)}), f32[384,384]{1,0:T(8,128)}) %all-reduce.3.cloned.1.call-update) | async-done | bytes 589840 | tf_op jit(solution)/shard_map/psum | solution.py:8
  61.6 0.0 all-reduce.5.cloned.1.call-update
  61.6 1.2 fusion.2
  62.8 56.6 %all-reduce.5.cloned.1.call-done = f32[384,384]{1,0:T(8,128)} async-done(((f32[384,384]{1,0:T(8,128)}), f32[384,384]{1,0:T(8,128)}) %all-reduce.5.cloned.1.call-update) | async-done | bytes 589840 | tf_op jit(solution)/shard_map/psum | solution.py:9
  119.3 1.1 neg.3
  120.4 1.1 copy.6
  121.5 2.7 %convolution_add_fusion = f32[512,384]{1,0:T(8,128)S(1)} fusion(f32[384,512]{1,0:T(8,128)S(1)} %fusion.2, f32[1,1,512,384]{3,2,1,0:T(8,128)S(1)} %copy-done.1, f32[384,384]{0,1:T(8,128)} %copy.6, s32[384]{0:T(512)S(1)} %iota_add_fusion, f32[384,384]{1,0:T(8,128)} %all-reduce.5.cloned.1.call-done), kind=kOutput, calls=%fused_computation.1 | convolution fusion | flops 454066176 | bytes 3540480 | tf_op jit(solution)/shard_map/dot_general | solution.py:13
  124.2 1.8 %convolution_bitcast_fusion = f32[1,1,512,384]{3,2,1,0:T(8,128)} fusion(f32[512,384]{1,0:T(8,128)S(1)} %convolution_add_fusion, f32[384,384]{1,0:T(8,128)S(1)} %fusion.5), kind=kOutput, calls=%fused_computation | convolution fusion | flops 452984832 | bytes 2162688 | tf_op jit(solution)/shard_map/dot_general | solution.py:13
  (1 shorter events, 0.0 us)
Async XLA Ops:
  6.5 12.6 %copy-start = (f32[1,1,512,384]{3,2,1,0:T(8,128)S(1)}, f32[1,1,512,384]{3,2,1,0:T(8,128)}, u32[]{:S(2)}) copy-start(f32[1,1,512,384]{3,2,1,0:T(8,128)} %param.6) | copy-start | bytes 2359300
  6.5 11.9 %copy-start.2 = (f32[1,1,384,384]{3,2,1,0:T(8,128)S(1)}, f32[1,1,384,384]{3,2,1,0:T(8,128)}, u32[]{:S(2)}) copy-start(f32[1,1,384,384]{3,2,1,0:T(8,128)} %param.8) | copy-start | bytes 1769476
  6.5 55.0 %all-reduce.3.cloned.1.call-start = ((), (), s32[]{:S(2)}) async-start(), calls=%async_computation | async-start | bytes 1179648 | tf_op jit(solution)/shard_map/psum | solution.py:8
  18.4 1.1 copy-start.1
  22.0 1.1 copy-start.3
  22.0 97.3 %all-reduce.5.cloned.1.call-start = ((), (), s32[]{:S(2)}) async-start(), calls=%async_computation.1 | async-start | bytes 1179648 | tf_op jit(solution)/shard_map/psum | solution.py:9
Sparse Core Ops, SparseCore 0:
  22.1 39.3 all-reduce.2
  64.7 54.5 all-reduce.4
